TPU v7x, 256 devices: a whole 4x4x8 slice. The times are simulated.
256 devices in a mesh: dp: 16 (over x_lo, z), shard: 16 (over x_hi, y, core).
Axes of the slice: x: 4 (x_hi: 2, x_lo: 2; x = x_hi * 2 + x_lo), y: 4, z: 8, core: 2. Of those that a mesh axis runs over, the one named last changes fastest.
Arguments:
- gradient: bfloat16 [16, 2560, 2560], P(None, ('shard', 'dp')), may hold values from -1.5 to 1.5
- owner: int32 [16], replicated, may hold values from 0 to 15, each once
- a_inverse: bfloat16 [16, 2560, 2560], P('dp', 'shard'), as said below
- b_inverse: bfloat16 [16, 2560, 2560], P('dp', 'shard'), as said below
Outputs:
- preconditioned: bfloat16 [16, 2560, 2560], P(None, ('shard', 'dp'))
Inputs may be any that keep to these rules, and one draw needn't show every extreme that they name: owner names each of the 16 slots for exactly one layer. Every slot of a_inverse is a symmetric matrix. Every slot of b_inverse is a symmetric matrix.
All inputs are finite; a program needn't handle non-finite values.
Results may differ from a plain program's by a relative error of at most 0.0049.
Values may be sent and summed in bfloat16 or wider, within the bound.
No kernel may reach another device: no remote copies, remote signals or barrier semaphores. Data moves between devices by JAX's collectives and lax.ppermute only.
A program may use at most 128 MiB of HBM per device.

v0:
```python
import jax
import jax.numpy as jnp
from jax import lax
from jax.sharding import PartitionSpec as P


def local(gradient, owner, a_inverse, b_inverse):
    layer_count = gradient.shape[0]
    chosen = (owner[:, None] == jnp.arange(layer_count, dtype=jnp.int32)[None, :]).astype(
        jnp.bfloat16
    )
    outgoing = jnp.einsum(
        "lo,lrc->orc", chosen, gradient, preferred_element_type=jnp.float32
    ).astype(jnp.bfloat16)
    owned = lax.all_to_all(outgoing, "dp", split_axis=0, concat_axis=1, tiled=True)
    grad_rows = owned[0]
    right_rows = b_inverse[0]
    left_rows = a_inverse[0]
    columns = grad_rows
    right_half = jnp.dot(
        columns,
        lax.all_gather(right_rows, "shard", axis=0, tiled=True),
        preferred_element_type=jnp.float32,
    ).astype(jnp.bfloat16)
    columns = left_rows
    summed = jnp.dot(
        columns,
        lax.all_gather(right_half, "shard", axis=0, tiled=True),
        preferred_element_type=jnp.float32,
    )
    result_rows = summed.astype(jnp.bfloat16)
    returned = lax.all_to_all(
        result_rows[None, :, :], "dp", split_axis=1, concat_axis=0, tiled=True
    )
    return jnp.take(returned, owner, axis=0)


def solution(mesh):
    in_specs = (P(None, ("shard", "dp"), None), P(), P("dp", "shard", None), P("dp", "shard", None))
    out_specs = P(None, ("shard", "dp"), None)
    return jax.shard_map(local, mesh=mesh, in_specs=in_specs, out_specs=out_specs, check_vma=False)
```

profile of v0, /device:TPU:32, one launch (start us, length us, event | category | flops | bytes accessed | tf_op | source)
XLA Modules:
  0.0 281.3 jit_solution(5845131515558374198)
XLA Ops:
  6.5 0.7 all-gather.6.cloned.1.call-update
  7.3 0.0 all-gather.4.cloned.1.call-start
  7.3 0.4 copy-done
  7.7 1.0 convolution_convert_fusion.1
  8.7 0.5 copy.7
  9.2 42.1 %all_to_all.21 = bf16[16,10,2560]{2,1,0:T(8,128)(2,1)S(1)} all-to-all(bf16[16,10,2560]{2,1,0:T(8,128)(2,1)S(1)} %copy.7), channel_id=1, replica_groups=mesh['dp'=16,'shard'=16] {'dp'}, dimensions={0} | all-to-all | bytes 1638400 | tf_op jit(solution)/shard_map/all_to_all | solution.py:15
  51.3 0.3 squeeze.9
  51.6 66.0 %all-gather.6.cloned.1.call-done = bf16[1,2560,2560]{2,1,0:T(8,128)(2,1)} async-done(((bf16[1,160,2560]{2,1,0:T(8,128)(2,1)}), bf16[1,2560,2560]{2,1,0:T(8,128)(2,1)}) %all-gather.6.cloned.1.call-update) | async-done | bytes 13107216 | tf_op jit(solution)/shard_map/all_gather | solution.py:22
  117.6 7.9 %fusion.2 = bf16[160,2560]{1,0:T(8,128)(2,1)} fusion(bf16[160,2560]{1,0:T(8,128)(2,1)S(1)} %squeeze.9, bf16[1,2560,2560]{2,1,0:T(8,128)(2,1)} %all-gather.6.cloned.1.call-done), kind=kOutput, calls=%fused_computation.3 | convolution fusion | flops 2097561600 | bytes 14745600 | tf_op jit(solution)/shard_map/dot_general | solution.py:20
  125.5 0.0 all-gather.4.cloned.1.call-update
  125.5 95.9 %all-gather.4.cloned.1.call-done = bf16[2560,2560]{1,0:T(8,128)(2,1)} async-done(((bf16[160,2560]{1,0:T(8,128)(2,1)}), bf16[2560,2560]{1,0:T(8,128)(2,1)}) %all-gather.4.cloned.1.call-update) | async-done | bytes 13107216 | tf_op jit(solution)/shard_map/all_gather | solution.py:28
  221.5 7.0 %fusion.5 = bf16[1,160,2560]{2,1,0:T(8,128)(2,1)S(1)} fusion(bf16[2560,2560]{1,0:T(8,128)(2,1)} %all-gather.4.cloned.1.call-done, bf16[1,160,2560]{2,1,0:T(8,128)(2,1)S(1)} %copy-done.2), kind=kOutput, calls=%fused_computation.6 | convolution fusion | flops 2097561600 | bytes 14745600 | tf_op jit(solution)/shard_map/dot_general | solution.py:26
  228.5 1.3 copy.12
  229.8 0.5 broadcast.17
  230.3 5.6 %reduce.2 = bf16[160,2560]{1,0:T(8,128)(2,1)S(1)} reduce(bf16[160,1,2560]{2,1,0:T(2,128)(2,1)S(1)} %bitcast.23, bf16[]{:T(256)} %broadcast.17), dimensions={1}, to_apply=%bitcast.22.reduce_sub_computation | reduce | bytes 1638402
  235.9 1.3 reshape.25
  237.2 7.5 %all-to-all-start.1 = ((bf16[16,2,12800]{2,1,0:T(2,128)(2,1)}), bf16[16,2,12800]{2,1,0:T(2,128)(2,1)S(1)}, u32[]{:S(2)}, u32[]{:S(2)}) async-start(bf16[16,2,12800]{2,1,0:T(2,128)(2,1)} %reshape.25), calls=%async_computation.1 | async-start | bytes 1638400 | tf_op jit(solution)/shard_map/all_to_all | solution.py:32
  244.7 21.8 %all-to-all-done.1 = bf16[16,2,12800]{2,1,0:T(2,128)(2,1)S(1)} async-done(((bf16[16,2,12800]{2,1,0:T(2,128)(2,1)}), bf16[16,2,12800]{2,1,0:T(2,128)(2,1)S(1)}, u32[]{:S(2)}, u32[]{:S(2)}) %all-to-all-start.1) | async-done | bytes 819232 | tf_op jit(solution)/shard_map/all_to_all | solution.py:32
  266.6 0.7 reshape.26
  267.2 4.7 %bitcast_reduce_fusion = bf16[160,2560]{1,0:T(8,128)(2,1)S(1)} fusion(bf16[160,1,2560]{2,1,0:T(2,128)(2,1)S(1)} %reshape.26), kind=kLoop, calls=%fused_computation.15 | loop fusion | bytes 1638400 | tf_op jit(solution)/shard_map/all_to_all | solution.py:32
  271.9 0.3 all_to_all.8
  272.3 0.6 gather_fusion
  272.9 0.2 broadcast_select_fusion
  273.1 1.3 copy.9
  (9 shorter events, 0.0 us)
Async XLA Ops:
  6.5 1.1 copy-start
  6.5 111.1 %all-gather.6.cloned.1.call-start = ((), (), s32[]{:S(2)}) async-start(), calls=%async_computation.3 | async-start | bytes 13926400 | tf_op jit(solution)/shard_map/all_gather | solution.py:22
  7.3 214.2 %all-gather.4.cloned.1.call-start = ((), (), s32[]{:S(2)}) async-start(), calls=%async_computation.2 | async-start | bytes 13926400 | tf_op jit(solution)/shard_map/all_gather | solution.py:28
  51.6 169.9 %copy-start.2 = (bf16[1,160,2560]{2,1,0:T(8,128)(2,1)S(1)}, bf16[1,160,2560]{2,1,0:T(8,128)(2,1)}, u32[]{:S(2)}) copy-start(bf16[1,160,2560]{2,1,0:T(8,128)(2,1)} %param.6) | copy-start | bytes 2457604
  235.9 8.8 %copy-start.1 = (s32[16]{0:T(128)S(1)}, s32[16]{0:T(128)}, u32[]{:S(2)}) copy-start(s32[16]{0:T(128)} %param.5) | copy-start | bytes 196
  237.2 29.4 %all-to-all-start.1 = ((bf16[16,2,12800]{2,1,0:T(2,128)(2,1)}), bf16[16,2,12800]{2,1,0:T(2,128)(2,1)S(1)}, u32[]{:S(2)}, u32[]{:S(2)}) async-start(bf16[16,2,12800]{2,1,0:T(2,128)(2,1)} %reshape.25), calls=%async_computation.1 | async-start | bytes 1638400 | tf_op jit(solution)/shard_map/all_to_all | solution.py:32
Sparse Core Ops, SparseCore 0:
  10.1 107.4 all-gather.5
  125.7 95.7 all-gather.3
where the time goes:
time: 282 us; the launch traced here: 281 us
  waiting for transfers between devices  185 us (66%)
  blocking collectives  42.1 us (15%)
  matrix products  15.9 us (6%)
  between operations  13.5 us (5%)
  local copies, waits for them, and re-layouts  11.9 us (4%)
  starting transfers between devices  7.54 us (3%)
  other arithmetic  5.81 us (2%)
    all_gather x1, waiting for transfers between devices, local(): lax.all_gather(right_half, 'shard', axis=0, tiled=True)  95.9 us
    all_gather x1, waiting for transfers between devices, local(): lax.all_gather(right_rows, 'shard', axis=0, tiled=True)  66 us
    all_to_all x1, blocking collectives, local(): lax.all_to_all(outgoing, 'dp', split_axis=0, concat_axis=1, tiled=True)  42.1 us
    all_to_all x1, waiting for transfers between devices, local(): lax.all_to_all(result_rows[None, :, :], 'dp', split_axis=1, concat_axis=0...  21.8 us
    dot_general x1, matrix products, local(): jnp.dot(columns, lax.all_gather(right_rows, 'shard', axis=0, tiled=True),...  7.9 us
    all_to_all x1, starting transfers between devices, local(): lax.all_to_all(result_rows[None, :, :], 'dp', split_axis=1, concat_axis=0...  7.5 us
    dot_general x1, matrix products, local(): jnp.dot(columns, lax.all_gather(right_half, 'shard', axis=0, tiled=True),...  7 us
  transfers between devices with their start and end apart: 3, of which 3 were waited for; matrix products, arithmetic and copies ran while one was open for 1% of the time, Pallas kernels for 0%

commit v1 on v0

--- a/solution.py
+++ b/solution.py
@@ -2,6 +2,15 @@
 import jax.numpy as jnp
 from jax import lax
 from jax.sharding import PartitionSpec as P
+
+
+def bind_halves(local_block, axis_tag, dim_at=0):
+    vals = []
+    for _ in range(lax.axis_size(axis_tag)):
+        vals.append(local_block)
+    w1 = jnp.stack(vals, axis=0)
+    part_next = lax.all_to_all(w1, axis_tag, 0, 0)
+    return jnp.concatenate(part_next, axis=dim_at)
 
 
 def local(gradient, owner, a_inverse, b_inverse):
@@ -23,11 +32,7 @@
         preferred_element_type=jnp.float32,
     ).astype(jnp.bfloat16)
     columns = left_rows
-    summed = jnp.dot(
-        columns,
-        lax.all_gather(right_half, "shard", axis=0, tiled=True),
-        preferred_element_type=jnp.float32,
-    )
+    summed = jnp.dot(columns, bind_halves(right_half, "shard"), preferred_element_type=jnp.float32)
     result_rows = summed.astype(jnp.bfloat16)
     returned = lax.all_to_all(
         result_rows[None, :, :], "dp", split_axis=1, concat_axis=0, tiled=True

time: 282 us -> 336 us (1.19)
  blocking collectives: 42.1 us -> 193 us
  waiting for transfers between devices: 185 us -> 87.7 us
  local copies, waits for them, and re-layouts: 11.9 us -> 17.8 us
  matrix products: 15.9 us -> 10.3 us
    all_to_all x0 -> x1, blocking collectives: none -> 151 us  [bind_halves(): part_next = lax.all_to_all(w1, axis_tag, 0, 0)]
    all_gather x1 -> x0, waiting for transfers between devices: 95.9 us -> none  [local(): lax.all_gather(right_half, 'shard', axis=0, tiled=True)]
    another operation x0 -> x1, local copies, waits for them, and re-layouts: none -> 5.93 us  [bind_halves(): w1 = jnp.stack(vals, axis=0)]
    dot_general x1, matrix products: 7 us -> 2.28 us  [local(): jnp.dot(columns, bind_halves(right_half, 'shard'), preferred_element_type...]
  transfers between devices with their start and end apart: 3 -> 2, of which waited for: 3 -> 2; matrix products, arithmetic and copies ran while one was open for 1% -> 1% of each run, Pallas kernels for 0% -> 0%
where the time goes in v1:
time: 336 us
  blocking collectives  193 us (57%)
  waiting for transfers between devices  87.7 us (26%)
  local copies, waits for them, and re-layouts  17.8 us (5%)
  between operations  13.5 us (4%)
  matrix products  10.3 us (3%)
  starting transfers between devices  7.51 us (2%)
  other arithmetic  5.81 us (2%)
    all_to_all x1, blocking collectives, bind_halves(): part_next = lax.all_to_all(w1, axis_tag, 0, 0)  151 us
    all_gather x1, waiting for transfers between devices, local(): lax.all_gather(right_rows, 'shard', axis=0, tiled=True)  66 us
    all_to_all x1, blocking collectives, local(): lax.all_to_all(outgoing, 'dp', split_axis=0, concat_axis=1, tiled=True)  42.1 us
    all_to_all x1, waiting for transfers between devices, local(): lax.all_to_all(result_rows[None, :, :], 'dp', split_axis=1, concat_axis=0...  20.9 us
    all_to_all x1, starting transfers between devices, local(): lax.all_to_all(result_rows[None, :, :], 'dp', split_axis=1, concat_axis=0...  7.51 us
    dot_general x1, matrix products, local(): jnp.dot(columns, lax.all_gather(right_rows, 'shard', axis=0, tiled=True),...  7 us
  transfers between devices with their start and end apart: 2, of which 2 were waited for; matrix products, arithmetic and copies ran while one was open for 1% of the time, Pallas kernels for 0%

profile of v1, /device:TPU:32, one launch (start us, length us, event | category | flops | bytes accessed | tf_op | source)
XLA Modules:
  0.0 335.9 jit_solution(12136196975475946362)
XLA Ops:
  6.5 0.7 all-gather.3.cloned.1.call-update
  7.3 0.4 copy-done
  7.7 1.0 convolution_convert_fusion.1
  8.7 0.5 copy.7
  9.2 42.1 %all_to_all.26 = bf16[16,10,2560]{2,1,0:T(8,128)(2,1)S(1)} all-to-all(bf16[16,10,2560]{2,1,0:T(8,128)(2,1)S(1)} %copy.7), channel_id=1, replica_groups=mesh['dp'=16,'shard'=16] {'dp'}, dimensions={0} | all-to-all | bytes 1638400 | tf_op jit(solution)/shard_map/all_to_all | solution.py:24
  51.3 0.3 squeeze.9
  51.6 66.0 %all-gather.3.cloned.1.call-done = bf16[1,2560,2560]{2,1,0:T(8,128)(2,1)} async-done(((bf16[1,160,2560]{2,1,0:T(8,128)(2,1)}), bf16[1,2560,2560]{2,1,0:T(8,128)(2,1)}) %all-gather.3.cloned.1.call-update) | async-done | bytes 13107216 | tf_op jit(solution)/shard_map/all_gather | solution.py:31
  117.6 7.0 %fusion.2 = bf16[160,2560]{1,0:T(8,128)(2,1)S(1)} fusion(bf16[160,2560]{1,0:T(8,128)(2,1)S(1)} %squeeze.9, bf16[1,2560,2560]{2,1,0:T(8,128)(2,1)} %all-gather.3.cloned.1.call-done), kind=kOutput, calls=%fused_computation.3 | convolution fusion | flops 2097561600 | bytes 14745600 | tf_op jit(solution)/shard_map/dot_general | solution.py:29
  124.6 5.9 %stack.2 = bf16[16,160,2560]{2,1,0:T(8,128)(2,1)} broadcast(bf16[160,2560]{1,0:T(8,128)(2,1)S(1)} %fusion.2), dimensions={1,2} | broadcast | bytes 13926400 | tf_op jit(solution)/shard_map/stack | solution.py:11
  130.6 151.2 %all_to_all.27 = bf16[16,160,2560]{2,1,0:T(8,128)(2,1)S(1)} all-to-all(bf16[16,160,2560]{2,1,0:T(8,128)(2,1)} %stack.2), channel_id=1, replica_groups=mesh['dp'=16,'shard'=16] {'shard'}, dimensions={0} | all-to-all | bytes 26214400 | tf_op jit(solution)/shard_map/all_to_all | solution.py:12
  281.8 2.3 fusion.5
  284.1 1.3 copy.12
  285.4 0.5 broadcast.19
  285.9 5.6 %reduce.2 = bf16[160,2560]{1,0:T(8,128)(2,1)S(1)} reduce(bf16[160,1,2560]{2,1,0:T(2,128)(2,1)S(1)} %bitcast.25, bf16[]{:T(256)} %broadcast.19), dimensions={1}, to_apply=%bitcast.23.reduce_sub_computation | reduce | bytes 1638402
  291.5 0.0 copy-start.1
  291.5 1.3 reshape.31
  292.8 7.5 %all-to-all-start.2 = ((bf16[16,2,12800]{2,1,0:T(2,128)(2,1)}), bf16[16,2,12800]{2,1,0:T(2,128)(2,1)S(1)}, u32[]{:S(2)}, u32[]{:S(2)}) async-start(bf16[16,2,12800]{2,1,0:T(2,128)(2,1)} %reshape.31), calls=%async_computation.2 | async-start | bytes 1638400 | tf_op jit(solution)/shard_map/all_to_all | solution.py:37
  300.3 20.9 %all-to-all-done.2 = bf16[16,2,12800]{2,1,0:T(2,128)(2,1)S(1)} async-done(((bf16[16,2,12800]{2,1,0:T(2,128)(2,1)}), bf16[16,2,12800]{2,1,0:T(2,128)(2,1)S(1)}, u32[]{:S(2)}, u32[]{:S(2)}) %all-to-all-start.2) | async-done | bytes 819232 | tf_op jit(solution)/shard_map/all_to_all | solution.py:37
  321.2 0.7 reshape.32
  321.9 4.7 %bitcast_reduce_fusion = bf16[160,2560]{1,0:T(8,128)(2,1)S(1)} fusion(bf16[160,1,2560]{2,1,0:T(2,128)(2,1)S(1)} %reshape.32), kind=kLoop, calls=%fused_computation.15 | loop fusion | bytes 1638400 | tf_op jit(solution)/shard_map/all_to_all | solution.py:37
  326.6 0.3 all_to_all.22
  326.9 0.6 gather_fusion
  327.6 0.2 broadcast_select_fusion
  327.8 1.3 copy.9
  (8 shorter events, 0.0 us)
Async XLA Ops:
  6.5 1.1 copy-start
  6.5 111.1 %all-gather.3.cloned.1.call-start = ((), (), s32[]{:S(2)}) async-start(), calls=%async_computation.3 | async-start | bytes 13926400 | tf_op jit(solution)/shard_map/all_gather | solution.py:31
  130.6 151.2 %copy-start.2 = (bf16[1,160,2560]{2,1,0:T(8,128)(2,1)S(1)}, bf16[1,160,2560]{2,1,0:T(8,128)(2,1)}, u32[]{:S(2)}) copy-start(bf16[1,160,2560]{2,1,0:T(8,128)(2,1)} %param.6) | copy-start | bytes 2457604
  291.5 8.8 %copy-start.1 = (s32[16]{0:T(128)S(1)}, s32[16]{0:T(128)}, u32[]{:S(2)}) copy-start(s32[16]{0:T(128)} %param.5) | copy-start | bytes 196
  292.8 28.5 %all-to-all-start.2 = ((bf16[16,2,12800]{2,1,0:T(2,128)(2,1)}), bf16[16,2,12800]{2,1,0:T(2,128)(2,1)S(1)}, u32[]{:S(2)}, u32[]{:S(2)}) async-start(bf16[16,2,12800]{2,1,0:T(2,128)(2,1)} %reshape.31), calls=%async_computation.2 | async-start | bytes 1638400 | tf_op jit(solution)/shard_map/all_to_all | solution.py:37
Sparse Core Ops, SparseCore 0:
  10.1 107.4 all-gather.2
